TPU v7x, 32 devices: a whole 2x2x4 slice. The times are simulated.
32 devices in a mesh: feat: 8 (over z, y), pair: 4 (over x, core).
Axes of the slice: x: 2, y: 2, z: 4, core: 2. Of those that a mesh axis runs over, the one named last changes fastest.
Arguments:
- in_factors: bfloat16 [512, 2, 512, 256], P(('feat', 'pair')), may hold values from -6 to 6
- out_factors: bfloat16 [512, 2, 512, 256], P(('feat', 'pair')), may hold values from -0.26367188 to 0.26367188
- token_counts: int32 [512, 2], P(('feat', 'pair')), may hold values from 1 to 512, as said below
- slot_pair: int32 [4, 128], P('pair'), may hold values from 0 to 127, each once within a row
- factor_panels: float32 [65536, 1536], P('feat'), as said below
Outputs:
- reduced: float32 [512, 65536], P('pair', 'feat')
Inputs may be any that keep to these rules, and one draw needn't show every extreme that they name: `token_counts`: column 0 counts the chosen response's tokens, column 1 the rejected one's; positions at or beyond the count are padding. `slot_pair`: each row is a permutation of 0 to 127. `factor_panels`: entries above the diagonal in the unknowns' order are zero: rows of panel j hold zeros in the columns of panels after j, and D_k has a positive diagonal.
All inputs are finite; a program needn't handle non-finite values.
Results may differ from a plain program's by a relative error of at most 0.0003.
Values sent between devices are 32-bit elements; how exact they have to be, the bound alone decides.
A program may use at most 128 MiB of HBM per device.

v0:
```python
import jax
import jax.numpy as jnp
from jax import lax
from jax.sharding import PartitionSpec as P

PANEL = 512
PANELS = 3


def spread(value, axis, source):
    kept = jnp.where(lax.axis_index(axis) == source, value, 0).astype(value.dtype)
    return lax.psum(kept, axis)


def panel_product(solved, panel_cols):
    return lax.dot_general(
        solved,
        panel_cols,
        (((1,), (1,)), ((), ())),
        precision=lax.Precision.HIGHEST,
        preferred_element_type=jnp.float32,
    )


def per_device(in_factors, out_factors, token_counts, slot_pair, factor_panels):
    slot_count, side_count, token_depth, proj_rank = in_factors.shape
    n_pair = lax.axis_size("pair")
    n_feat = lax.axis_size("feat")
    per_group = slot_count // n_pair
    row_count = factor_panels.shape[0]
    feat_index = lax.axis_index("feat")
    positions = lax.broadcasted_iota(jnp.int32, (slot_count, side_count, token_depth), 2)
    side_index = lax.broadcasted_iota(jnp.int32, (slot_count, side_count, token_depth), 1)
    weights = jnp.where(
        positions < token_counts[:, :, None], jnp.where(side_index == 0, 1.0, -1.0), 0.0
    ).astype(jnp.bfloat16)
    signed = out_factors * weights[..., None]
    gradients = jnp.einsum("ksti,kstj->kij", signed, in_factors, preferred_element_type=jnp.float32)
    gradients = gradients.reshape(n_pair, per_group, n_feat, row_count)
    group_pairs = slot_pair[0]
    pair_total = n_pair * n_feat * per_group
    outgoing = gradients.transpose(2, 0, 1, 3).reshape(n_feat * n_pair, per_group, row_count)
    received = lax.all_to_all(
        outgoing, ("feat", "pair"), split_axis=0, concat_axis=1, tiled=True
    ).reshape(pair_total, row_count)
    pair_rows = lax.broadcasted_iota(jnp.int32, (pair_total, pair_total), 0)
    placement = (pair_rows == group_pairs[None, :]).astype(jnp.float32)
    right_side = jnp.dot(
        placement, received, precision=lax.Precision.HIGHEST, preferred_element_type=jnp.float32
    )
    identity = jnp.eye(PANEL, dtype=jnp.float32)

    def solve_panel(k, current):
        diagonal = jnp.where(
            feat_index == k, factor_panels[:PANEL, k * PANEL : (k + 1) * PANEL], identity
        )
        solved = jax.scipy.linalg.solve_triangular(diagonal, current[:, :PANEL].T, lower=True).T
        return spread(solved, "feat", k)

    solved = solve_panel(0, right_side)
    for k in range(PANELS):
        panel_cols = factor_panels[:, k * PANEL : (k + 1) * PANEL]
        head_rows = right_side[:, :PANEL] - panel_product(solved, panel_cols[:PANEL])
        head_rows = jnp.where(feat_index == k, solved, head_rows)
        following = solved
        if k + 1 < PANELS:
            following = solve_panel(k + 1, head_rows)
        tail_rows = right_side[:, PANEL:] - panel_product(solved, panel_cols[PANEL:])
        right_side = jnp.concatenate([head_rows, tail_rows], axis=1)
        solved = following
    return right_side


def solution(mesh):
    return jax.shard_map(
        per_device,
        mesh=mesh,
        in_specs=(
            P(("feat", "pair"), None, None, None),
            P(("feat", "pair"), None, None, None),
            P(("feat", "pair"), None),
            P("pair", None),
            P("feat", None),
        ),
        out_specs=P("pair", "feat"),
        check_vma=False,
    )
```

profile of v0, /device:TPU:24, one launch (start us, length us, event | category | flops | bytes accessed | tf_op | source)
XLA Modules:
  0.0 416.8 jit_solution(17209154780739720358)
XLA Ops:
  6.5 0.8 copy.20
  7.4 9.8 %fusion.18 = f32[16,256,256]{2,1,0:T(8,128)} fusion(bf16[16,2,512,256]{3,2,1,0:T(8,128)(2,1)} %param.7, bf16[16,2,512,256]{3,2,1,0:T(8,128)(2,1)} %param.8, bf16[16,2,512]{2,1,0:T(2,128)(2,1)S(1)} %fusion.63), kind=kOutput, calls=%fused_computation.19 | convolution fusion | flops 2151677952 | bytes 21004288 | tf_op jit(solution)/shard_map/ksti,kstj->kij/dot_general | solution.py:38
  17.3 5.0 %reshape.28 = f32[4,4,8,8192]{3,2,1,0:T(8,128)} reshape(f32[16,256,256]{2,1,0:T(8,128)} %fusion.18) | data formatting | bytes 8388608 | tf_op jit(solution)/shard_map/reshape | solution.py:39
  22.2 6.9 %copy.22 = f32[4,4,8,8192]{3,1,0,2:T(4,128)} copy(f32[4,4,8,8192]{3,2,1,0:T(8,128)} %reshape.28) | data formatting | bytes 8388608 | tf_op jit(solution)/shard_map/reshape | solution.py:39
  29.1 5.9 %all-to-all-start = ((f32[32,4,8192]{2,1,0:T(4,128)}), f32[32,4,8192]{2,1,0:T(4,128)}, u32[]{:S(2)}, u32[]{:S(2)}) async-start(f32[32,4,8192]{2,1,0:T(4,128)} %bitcast.103), calls=%async_computation | async-start | bytes 8388608 | tf_op jit(solution)/shard_map/all_to_all | solution.py:43
  35.3 2.3 fusion.24
  37.6 8.4 %while.6 = (s32[]{:T(128)}, f32[512,512]{1,0:T(8,128)S(1)}, s32[4,2]{0,1:T(2,128)S(1)}, f32[4,128,128]{2,1,0:T(8,128)S(1)}, s32[]{:T(128)}) while((s32[]{:T(128)}, f32[512,512]{1,0:T(8,128)S(1)}, s32[4,2]{0,1:T(2,128)S(1)}, f32[4,128,128]{2,1,0:T(8,128)S(1)}, s32[]{:T(128)}) %tuple.51), condition=%wide.while_cond, body=%wide.while_body.sunk | while | flops 2 | bytes 131189 | solution.py:57
  37.7 0.6 fusion.116
  38.3 1.4 bitcast_dynamic-update-slice_fusion.6
  39.8 0.6 fusion.116
  40.4 1.4 bitcast_dynamic-update-slice_fusion.6
  41.9 0.6 fusion.116
  42.5 1.4 bitcast_dynamic-update-slice_fusion.6
  44.0 0.6 fusion.116
  44.6 1.4 bitcast_dynamic-update-slice_fusion.6
  46.0 0.7 copy-done.4
  46.7 40.1 %custom-call.5 = f32[4,128,128]{1,2,0:T(8,128)S(1)} custom-call(f32[4,128,128]{2,1,0:T(8,128)} %copy-done.4), custom_call_target="InvertDiagBlocksLowerTriangular" | custom-call | tf_op jit(solution)/shard_map/jit(_solve_triangular)/triangular_solve | solution.py:57
  86.9 0.8 broadcast.62.clone.1
  87.6 9.7 %while.7 = (s32[]{:T(128)}, f32[512,512]{1,0:T(8,128)S(1)}, s32[4,2]{0,1:T(2,128)S(1)}, f32[4,128,128]{2,1,0:T(8,128)}, s32[]{:T(128)}) while((s32[]{:T(128)}, f32[512,512]{1,0:T(8,128)S(1)}, s32[4,2]{0,1:T(2,128)S(1)}, f32[4,128,128]{2,1,0:T(8,128)}, s32[]{:T(128)}) %tuple.66), condition=%wide.while_cond.clone, body=%wide.while_body.clone.sunk | while | flops 2 | bytes 132205 | solution.py:57
  87.7 0.5 fusion.117
  88.2 1.8 bitcast_dynamic-update-slice_fusion.7
  90.1 0.5 fusion.117
  90.7 1.8 bitcast_dynamic-update-slice_fusion.7
  92.6 0.5 fusion.117
  93.1 1.8 bitcast_dynamic-update-slice_fusion.7
  95.0 0.5 fusion.117
  95.5 1.8 bitcast_dynamic-update-slice_fusion.7
  97.3 30.2 %all-to-all-done = f32[32,4,8192]{2,1,0:T(4,128)} async-done(((f32[32,4,8192]{2,1,0:T(4,128)}), f32[32,4,8192]{2,1,0:T(4,128)}, u32[]{:S(2)}, u32[]{:S(2)}) %all-to-all-start) | async-done | bytes 4194336 | tf_op jit(solution)/shard_map/all_to_all | solution.py:43
  127.5 5.3 %reshape.30 = f32[128,8192]{1,0:T(8,128)} reshape(f32[32,4,8192]{2,1,0:T(4,128)} %all-to-all-done) | data formatting | bytes 8388608 | tf_op jit(solution)/shard_map/reshape | solution.py:45
  132.8 4.5 %fusion.82 = f32[128,8192]{1,0:T(8,128)S(1)} fusion(f32[128,8192]{1,0:T(8,128)} %reshape.30, s32[128]{0:T(128)S(1)} %bitcast.112), kind=kOutput, calls=%fused_computation.116 | convolution fusion | flops 1610629120 | bytes 8389120 | tf_op jit(solution)/shard_map/dot_general | solution.py:48
  137.4 2.0 copy-done
  140.3 0.4 convolution_subtract_fusion.7
  140.7 1.1 fusion.77
  141.8 0.5 convolution_subtract_fusion.11
  142.6 1.0 fusion.76
  143.6 0.7 fusion.30
  144.7 7.8 %while.8 = (s32[]{:T(128)}, f32[512,512]{1,0:T(8,128)S(1)}, s32[4,2]{0,1:T(2,128)S(1)}, f32[4,128,128]{2,1,0:T(8,128)S(1)}, s32[]{:T(128)}) while((s32[]{:T(128)}, f32[512,512]{1,0:T(8,128)S(1)}, s32[4,2]{0,1:T(2,128)S(1)}, f32[4,128,128]{2,1,0:T(8,128)S(1)}, s32[]{:T(128)}) %tuple.67), condition=%wide.while_cond.clone.1, body=%wide.while_body.clone.1.sunk | while | flops 2 | bytes 131189 | solution.py:57
  144.8 0.6 fusion.118
  145.4 1.3 bitcast_dynamic-update-slice_fusion.8
  146.7 0.6 fusion.118
  147.3 1.3 bitcast_dynamic-update-slice_fusion.8
  148.7 0.6 fusion.118
  149.3 1.3 bitcast_dynamic-update-slice_fusion.8
  150.6 0.6 fusion.118
  151.2 1.3 bitcast_dynamic-update-slice_fusion.8
  152.5 40.1 %custom-call.6 = f32[4,128,128]{1,2,0:T(8,128)S(1)} custom-call(f32[4,128,128]{2,1,0:T(8,128)} %get-tuple-element.27), custom_call_target="InvertDiagBlocksLowerTriangular" | custom-call | tf_op jit(solution)/shard_map/jit(_solve_triangular)/triangular_solve | solution.py:57
  192.6 39.3 %custom-call.7 = f32[4,128,128]{1,2,0:T(8,128)S(1)} custom-call(f32[4,128,128]{2,1,0:T(8,128)S(1)} %get-tuple-element.28), custom_call_target="InvertDiagBlocksLowerTriangular" | custom-call | tf_op jit(solution)/shard_map/jit(_solve_triangular)/triangular_solve | solution.py:57
  232.0 2.6 fusion.23
  234.9 0.3 convolution_subtract_fusion.6
  235.5 0.4 convolution_subtract_fusion.5
  236.2 0.5 convolution_subtract_fusion.10
  237.2 0.7 fusion.31
  238.0 0.3 all-reduce.8.cloned.1.call-start
  238.3 21.2 %fusion.6 = f32[128,7680]{1,0:T(8,128)} fusion(f32[128,512]{1,0:T(8,128)S(1)} %copy-done.1, f32[8192,1536]{1,0:T(8,128)} %param.11, f32[128,8192]{1,0:T(8,128)} %copy-done), kind=kOutput, calls=%fused_computation.12 | convolution fusion | flops 6040780800 | bytes 23855104 | tf_op jit(solution)/shard_map/dot_general | solution.py:16
  259.5 49.2 %all-reduce.6.cloned.1.call-done = f32[128,512]{1,0:T(8,128)} async-done(((f32[128,512]{1,0:T(8,128)}), f32[128,512]{1,0:T(8,128)}) %all-reduce.6.cloned.1.call-update) | async-done | bytes 262160 | tf_op jit(solution)/shard_map/psum | solution.py:12
  308.7 2.6 fusion.22
  312.1 0.4 convolution_subtract_fusion.3
  312.8 0.5 convolution_subtract_fusion.9
  313.8 0.7 fusion.32
  314.6 23.2 %fusion.9 = f32[128,7680]{1,0:T(8,128)} fusion(f32[128,7680]{1,0:T(8,128)} %fusion.6, f32[128,512]{1,0:T(8,128)S(1)} %copy-done.2, f32[8192,1536]{1,0:T(8,128)} %param.11), kind=kOutput, calls=%fused_computation.13 | convolution fusion | flops 6040780800 | bytes 23855104 | tf_op jit(solution)/shard_map/dot_general | solution.py:16
  337.8 47.1 %all-reduce.8.cloned.1.call-done = f32[128,512]{1,0:T(8,128)} async-done(((f32[128,512]{1,0:T(8,128)}), f32[128,512]{1,0:T(8,128)}) %all-reduce.8.cloned.1.call-update) | async-done | bytes 262160 | tf_op jit(solution)/shard_map/psum | solution.py:12
  384.9 2.5 fusion.21
  387.5 20.4 %fusion.12 = f32[128,7680]{1,0:T(8,128)S(1)} fusion(f32[128,7680]{1,0:T(8,128)} %fusion.9, f32[128,512]{1,0:T(8,128)} %all-reduce.8.cloned.1.call-done, f32[8192,1536]{1,0:T(8,128)} %param.11), kind=kOutput, calls=%fused_computation.14 | convolution fusion | flops 6040780800 | bytes 23855104 | tf_op jit(solution)/shard_map/dot_general | solution.py:16
  407.8 2.3 pad_maximum_fusion
  (56 shorter events, 5.7 us)
Async XLA Ops:
  29.1 98.4 %all-to-all-start = ((f32[32,4,8192]{2,1,0:T(4,128)}), f32[32,4,8192]{2,1,0:T(4,128)}, u32[]{:S(2)}, u32[]{:S(2)}) async-start(f32[32,4,8192]{2,1,0:T(4,128)} %bitcast.103), calls=%async_computation | async-start | bytes 8388608 | tf_op jit(solution)/shard_map/all_to_all | solution.py:43
  35.0 196.9 %all-reduce.4.cloned.1.call-start = ((), (), s32[]{:S(2)}) async-start(), calls=%async_computation.1 | async-start | bytes 524288 | tf_op jit(solution)/shard_map/psum | solution.py:12
  46.0 0.7 copy-start.4
  86.9 53.1 %copy-start.3 = (f32[4,128,128]{1,2,0:T(8,128)}, f32[4,128,128]{1,2,0:T(8,128)S(1)}, u32[]{:S(2)}) copy-start(f32[4,128,128]{1,2,0:T(8,128)S(1)} %custom-call.5) | copy-start | bytes 786436
  97.3 35.5 %copy-start.5 = (s32[1,128]{1,0:T(1,128)S(1)}, s32[1,128]{1,0:T(1,128)}, u32[]{:S(2)}) copy-start(s32[1,128]{1,0:T(1,128)} %param.10) | copy-start | bytes 1540
  137.3 2.0 copy-start
  144.4 164.3 %all-reduce.6.cloned.1.call-start = ((), (), s32[]{:S(2)}) async-start(), calls=%async_computation.2 | async-start | bytes 524288 | tf_op jit(solution)/shard_map/psum | solution.py:12
  232.0 6.3 %copy-start.1 = (f32[128,512]{1,0:T(8,128)S(1)}, f32[128,512]{1,0:T(8,128)}, u32[]{:S(2)}) copy-start(f32[128,512]{1,0:T(8,128)} %all-reduce.4.cloned.1.call-done) | copy-start | bytes 786436
  238.0 147.0 %all-reduce.8.cloned.1.call-start = ((), (), s32[]{:S(2)}) async-start(), calls=%async_computation.3 | async-start | bytes 524288 | tf_op jit(solution)/shard_map/psum | solution.py:12
  308.7 5.9 %copy-start.2 = (f32[128,512]{1,0:T(8,128)S(1)}, f32[128,512]{1,0:T(8,128)}, u32[]{:S(2)}) copy-start(f32[128,512]{1,0:T(8,128)} %all-reduce.6.cloned.1.call-done) | copy-start | bytes 786436
Sparse Core Ops, SparseCore 0:
  144.5 72.4 all-reduce.3
  238.1 70.5 all-reduce.5
  314.7 70.1 all-reduce.7
where the time goes:
time: 425 us; the launch traced here: 417 us
  waiting for transfers between devices  127 us (30%)
  other arithmetic  126 us (30%)
  matrix products  95.2 us (22%)
  local copies, waits for them, and re-layouts  48 us (11%)
  between operations  13.7 us (3%)
  starting transfers between devices  6.68 us (2%)
    another operation x5, other arithmetic, solve_panel(): jax.scipy.linalg.solve_triangular(diagonal, current[:, :PANEL].T, lower=T...  122 us
    psum x3, waiting for transfers between devices, spread(): return lax.psum(kept, axis)  96.4 us
    dot_general x6, matrix products, panel_product(): lax.dot_general(solved, panel_cols, (((1,), (1,)), ((), ())), precision=l...  72.5 us
    all_to_all x1, waiting for transfers between devices, per_device(): lax.all_to_all(outgoing, ('feat', 'pair'), split_axis=0, concat_axis=1, t...  30.2 us
    another operation x49, local copies, waits for them, and re-layouts, solve_panel(): jax.scipy.linalg.solve_triangular(diagonal, current[:, :PANEL].T, lower=T...  27.4 us
    reshape x2, local copies, waits for them, and re-layouts, per_device(): gradients = gradients.reshape(n_pair, per_group, n_feat, row_count)  11.9 us
    dot_general x1, matrix products, per_device(): jnp.einsum('ksti,kstj->kij', signed, in_factors, preferred_element_type=j...  9.84 us
  transfers between devices with their start and end apart: 4, of which 3 were waited for; matrix products, arithmetic and copies ran while one was open for 46% of the time, Pallas kernels for 0%

commit v1 on v0

v1 whole, which is shorter than its diff:
```python
import functools

import jax
import jax.numpy as jnp
from jax import lax
from jax.experimental import pallas as pl
from jax.experimental.pallas import tpu as pltpu
from jax.sharding import PartitionSpec as P

PANEL = 512
PANELS = 3
CHUNKS = 4
NT = (((1,), (1,)), ((), ()))


def dot_exact(a, b):
    return lax.dot_general(
        a, b, NT, precision=lax.Precision.HIGHEST, preferred_element_type=jnp.float32
    )


def chain_kernel(n_feat, head_ref, inverse_ref, lead_ref, out_ref, held, send_sem, recv_sem):
    feat = lax.axis_index("feat")
    pair = lax.axis_index("pair")
    level = feat // 2
    levels = n_feat // 2
    partner = feat + 1 - 2 * lax.rem(feat, 2)
    rows = head_ref.shape[0] // CHUNKS

    barrier = pltpu.get_barrier_semaphore()

    def greet(target):
        pl.semaphore_signal(
            barrier, inc=1, device_id=(target, pair), device_id_type=pl.DeviceIdType.MESH
        )

    greet(partner)

    @pl.when(level > 0)
    def _():
        greet(feat - 2)

    @pl.when(level + 1 < levels)
    def _():
        greet(feat + 2)

    below = jnp.where(level > 0, 1, 0)
    above = jnp.where(level + 1 < levels, 1, 0)
    pl.semaphore_wait(barrier, 1 + below + above)

    def piece(k, c, way, target):
        part = held.at[pl.ds(c * rows, rows), pl.ds(k * PANEL, PANEL)]
        return pltpu.make_async_remote_copy(
            src_ref=part,
            dst_ref=part,
            send_sem=send_sem.at[k, c, way],
            recv_sem=recv_sem.at[k, c],
            device_id=(target, pair),
            device_id_type=pl.DeviceIdType.MESH,
        )

    def routes(k):
        top = k // 2
        return (
            (0, feat == k, partner),
            (1, (level >= top) & (level + 1 < levels), feat + 2),
            (2, (level <= top) & (level > 0), feat - 2),
        )

    for k in range(PANELS):

        @pl.when(feat == k)
        def _():
            current = head_ref[...]
            if k > 0:
                current = current - dot_exact(held[:, : k * PANEL], lead_ref[:, : k * PANEL])
            held[:, k * PANEL : (k + 1) * PANEL] = dot_exact(current, inverse_ref[...])

        for c in range(CHUNKS):

            @pl.when(feat != k)
            def _():
                piece(k, c, 0, partner).wait_recv()

            for way, active, target in routes(k):

                @pl.when(active)
                def _():
                    piece(k, c, way, target).start()

    out_ref[...] = held[...]
    for k in range(PANELS):
        for c in range(CHUNKS):
            for way, active, target in routes(k):

                @pl.when(active)
                def _():
                    piece(k, c, way, target).wait_send()


def solve_chain(head, inverse, lead, n_feat):
    pairs = head.shape[0]
    return pl.pallas_call(
        functools.partial(chain_kernel, n_feat),
        out_shape=jax.ShapeDtypeStruct((pairs, PANELS * PANEL), jnp.float32),
        in_specs=[pl.BlockSpec(memory_space=pltpu.VMEM)] * 3,
        out_specs=pl.BlockSpec(memory_space=pltpu.VMEM),
        scratch_shapes=[
            pltpu.VMEM((pairs, PANELS * PANEL), jnp.float32),
            pltpu.SemaphoreType.DMA((PANELS, CHUNKS, 3)),
            pltpu.SemaphoreType.DMA((PANELS, CHUNKS)),
        ],
        compiler_params=pltpu.CompilerParams(
            collective_id=0, has_side_effects=True, vmem_limit_bytes=40 * 1024 * 1024
        ),
    )(head, inverse, lead)


def per_device(in_factors, out_factors, token_counts, slot_pair, factor_panels):
    slot_count, side_count, token_depth, proj_rank = in_factors.shape
    n_pair = lax.axis_size("pair")
    n_feat = lax.axis_size("feat")
    per_group = slot_count // n_pair
    row_count = factor_panels.shape[0]
    block = row_count // proj_rank
    feat_index = lax.axis_index("feat")
    positions = lax.broadcasted_iota(jnp.int32, (slot_count, side_count, token_depth), 2)
    side_index = lax.broadcasted_iota(jnp.int32, (slot_count, side_count, token_depth), 1)
    weights = jnp.where(
        positions < token_counts[:, :, None], jnp.where(side_index == 0, 1.0, -1.0), 0.0
    ).astype(jnp.bfloat16)
    signed = out_factors * weights[..., None]
    gradients = jnp.einsum("ksti,kstj->kij", signed, in_factors, preferred_element_type=jnp.float32)
    gradients = gradients.reshape(n_pair, per_group, n_feat, block, proj_rank)
    group_pairs = slot_pair[0]
    pair_total = n_pair * n_feat * per_group
    outgoing = gradients.transpose(2, 0, 1, 3, 4).reshape(
        n_feat * n_pair, per_group, block, proj_rank
    )
    received = lax.all_to_all(
        outgoing, ("feat", "pair"), split_axis=0, concat_axis=1, tiled=True
    ).reshape(pair_total, row_count)

    own = jnp.minimum(feat_index, PANELS - 1)
    lead = factor_panels[:PANEL]
    identity = jnp.eye(PANEL, dtype=jnp.float32)
    diagonal = lax.dynamic_slice(lead, (0, own * PANEL), (PANEL, PANEL))
    diagonal = jnp.where(feat_index < PANELS, diagonal, identity)
    inverse = jax.scipy.linalg.solve_triangular(diagonal, identity, lower=True)

    pair_rows = lax.broadcasted_iota(jnp.int32, (pair_total, pair_total), 0)
    placement = (pair_rows == group_pairs[None, :]).astype(jnp.float32)
    right_side = jnp.dot(
        placement, received, precision=lax.Precision.HIGH, preferred_element_type=jnp.float32
    )
    solved = solve_chain(right_side[:, :PANEL], inverse, lead, n_feat)
    result = right_side - lax.dot_general(
        solved,
        factor_panels,
        NT,
        precision=lax.Precision.HIGH,
        preferred_element_type=jnp.float32,
    )
    own_solved = lax.dynamic_slice(solved, (0, own * PANEL), (pair_total, PANEL))
    head = jnp.where(feat_index < PANELS, own_solved, result[:, :PANEL])
    return lax.dynamic_update_slice(result, head, (0, 0))


def solution(mesh):
    return jax.shard_map(
        per_device,
        mesh=mesh,
        in_specs=(
            P(("feat", "pair"), None, None, None),
            P(("feat", "pair"), None, None, None),
            P(("feat", "pair"), None),
            P("pair", None),
            P("feat", None),
        ),
        out_specs=P("pair", "feat"),
        check_vma=False,
    )
```

time: 425 us -> 189 us (0.44); the launches traced: 417 us -> 186 us
  waiting for transfers between devices: 127 us -> 27.5 us
  other arithmetic: 126 us -> 44.3 us
  matrix products: 95.2 us -> 46.1 us
  Pallas kernels: 0 us -> 33.4 us
  local copies, waits for them, and re-layouts: 48 us -> 28.2 us
  between operations: 13.7 us -> 0.21 us
    psum x3 -> x0, waiting for transfers between devices: 96.4 us -> none  [spread(): return lax.psum(kept, axis)]
    another operation x5 -> x4, other arithmetic: 122 us -> 42.3 us  [per_device(): inverse = jax.scipy.linalg.solve_triangular(diagonal, identity, lower=True)]
    dot_general x7 -> x2, matrix products: 77 us -> 31.9 us  [the longest x1 30.5 us: per_device(): lax.dot_general(solved, factor_panels, NT, precision=lax.Precision.HIGH,...]
    pallas_call x0 -> x1, Pallas kernels: none -> 33.4 us  [solve_chain(): pl.pallas_call(functools.partial(chain_kernel, n_feat), out_shape=jax.Sha...]
    reshape x3 -> x1, local copies, waits for them, and re-layouts: 17.1 us -> 2.35 us  [per_device(): gradients = gradients.reshape(n_pair, per_group, n_feat, block, proj_rank)]
    another operation x49 -> x13, local copies, waits for them, and re-layouts: 27.4 us -> 14.6 us  [solve_panel(): jax.scipy.linalg.solve_triangular(diagonal, current[:, :PANEL].T, lower=T...]
    unnamed x13 -> x10, local copies, waits for them, and re-layouts: 3.47 us -> 9.15 us
  transfers between devices with their start and end apart: 4 -> 1, of which waited for: 3 -> 1; matrix products, arithmetic and copies ran while one was open for 46% -> 35% of each run, Pallas kernels for 0% -> 0%
where the time goes in v1:
time: 189 us; the launch traced here: 186 us
  matrix products  46.1 us (24%)
  other arithmetic  44.3 us (23%)
  Pallas kernels  33.4 us (18%)
  local copies, waits for them, and re-layouts  28.2 us (15%)
  waiting for transfers between devices  27.5 us (15%)
  starting transfers between devices  5.93 us (3%)
    another operation x4, other arithmetic, per_device(): inverse = jax.scipy.linalg.solve_triangular(diagonal, identity, lower=True)  42.3 us
    pallas_call x1, Pallas kernels, solve_chain(): pl.pallas_call(functools.partial(chain_kernel, n_feat), out_shape=jax.Sha...  33.4 us
    dot_general x1, matrix products, per_device(): lax.dot_general(solved, factor_panels, NT, precision=lax.Precision.HIGH,...  30.5 us
    all_to_all x1, waiting for transfers between devices, per_device(): lax.all_to_all(outgoing, ('feat', 'pair'), split_axis=0, concat_axis=1, t...  27.5 us
    another operation x12, local copies, waits for them, and re-layouts  14.6 us
    unnamed x10, local copies, waits for them, and re-layouts  9.15 us
    dot_general x1, matrix products, per_device(): jnp.einsum('ksti,kstj->kij', signed, in_factors, preferred_element_type=j...  8.54 us
    all_to_all x1, starting transfers between devices, per_device(): lax.all_to_all(outgoing, ('feat', 'pair'), split_axis=0, concat_axis=1, t...  5.93 us
  transfers between devices with their start and end apart: 1, of which 1 were waited for; matrix products, arithmetic and copies ran while one was open for 35% of the time, Pallas kernels for 0%

profile of v1, /device:TPU:24, one launch (start us, length us, event | category | flops | bytes accessed | tf_op | source)
XLA Modules:
  0.0 185.8 jit_solution(8572154914922841235)
XLA Ops:
  0.0 0.8 copy.8
  0.8 0.1 fusion.17
  0.9 8.5 %fusion = f32[16,256,256,1]{2,1,3,0:T(8,128)S(1)} fusion(bf16[16,2,512,256]{3,2,1,0:T(8,128)(2,1)} %param.5, bf16[16,2,512,256]{3,2,1,0:T(8,128)(2,1)} %param.6, bf16[16,2,512]{2,1,0:T(2,128)(2,1)S(1)} %fusion.17), kind=kOutput, calls=%fused_computation.3 | convolution fusion | flops 2151677952 | bytes 21004288 | tf_op jit(solution)/shard_map/ksti,kstj->kij/dot_general | solution.py:133
  9.4 2.3 %copy.10 = f32[4,4,8,32,256]{4,3,1,0,2:T(8,128)} copy(f32[4,4,8,32,256]{4,3,2,1,0:T(8,128)S(1)} %bitcast.43) | data formatting | bytes 8388608 | tf_op jit(solution)/shard_map/reshape | solution.py:134
  11.8 5.9 %all-to-all-start = ((f32[32,4,32,256]{3,2,1,0:T(8,128)}), f32[32,4,32,256]{3,2,1,0:T(8,128)}, u32[]{:S(2)}, u32[]{:S(2)}) async-start(f32[32,4,32,256]{3,2,1,0:T(8,128)} %bitcast.41), calls=%async_computation | async-start | bytes 8388608 | tf_op jit(solution)/shard_map/all_to_all | solution.py:140
  17.7 2.1 %slice.43.lead_ref = f32[512,1536]{1,0:T(8,128)S(1)} slice(f32[8192,1536]{1,0:T(8,128)} %param.9), slice={[0:512], [0:1536]} | slice | bytes 6291456 | tf_op jit(solution)/shard_map/slice | solution.py:145
  19.8 1.1 select_select_fusion
  21.0 14.6 %while.1 = (s32[]{:T(128)}, f32[512,512]{1,0:T(8,128)}, s32[4,2]{0,1:T(2,128)S(1)}, f32[4,128,128]{2,1,0:T(8,128)}, s32[]{:T(128)}) while((s32[]{:T(128)}, f32[512,512]{1,0:T(8,128)}, s32[4,2]{0,1:T(2,128)S(1)}, f32[4,128,128]{2,1,0:T(8,128)}, s32[]{:T(128)}) %tuple.19), condition=%wide.while_cond, body=%wide.while_body.sunk | while | flops 2 | bytes 132205 | solution.py:149
  21.0 0.1 constant_dynamic-slice_fusion.2
  21.0 0.6 fusion.36
  21.6 3.0 %bitcast_dynamic-update-slice_fusion.2 = f32[4,128,128]{2,1,0:T(8,128)} fusion(f32[4,128,128]{2,1,0:T(8,128)} %get-tuple-element.60, s32[]{:T(128)S(6)} %copy.17, f32[512,512]{1,0:T(8,128)} %get-tuple-element.63, s32[]{:T(128)} %bitcast.39, s32[]{:T(128)} %bitcast.40), kind=kLoop, calls=%fused_computation.clone.1 | loop fusion | bytes 132100 | tf_op jit(solution)/shard_map/jit(_solve_triangular)/triangular_solve
  24.6 0.1 constant_dynamic-slice_fusion.2
  24.7 0.6 fusion.36
  25.3 3.0 %bitcast_dynamic-update-slice_fusion.2 = f32[4,128,128]{2,1,0:T(8,128)} fusion(f32[4,128,128]{2,1,0:T(8,128)} %get-tuple-element.60, s32[]{:T(128)S(6)} %copy.17, f32[512,512]{1,0:T(8,128)} %get-tuple-element.63, s32[]{:T(128)} %bitcast.39, s32[]{:T(128)} %bitcast.40), kind=kLoop, calls=%fused_computation.clone.1 | loop fusion | bytes 132100 | tf_op jit(solution)/shard_map/jit(_solve_triangular)/triangular_solve
  28.3 0.1 constant_dynamic-slice_fusion.2
  28.4 0.6 fusion.36
  29.0 3.0 %bitcast_dynamic-update-slice_fusion.2 = f32[4,128,128]{2,1,0:T(8,128)} fusion(f32[4,128,128]{2,1,0:T(8,128)} %get-tuple-element.60, s32[]{:T(128)S(6)} %copy.17, f32[512,512]{1,0:T(8,128)} %get-tuple-element.63, s32[]{:T(128)} %bitcast.39, s32[]{:T(128)} %bitcast.40), kind=kLoop, calls=%fused_computation.clone.1 | loop fusion | bytes 132100 | tf_op jit(solution)/shard_map/jit(_solve_triangular)/triangular_solve
  32.0 0.1 constant_dynamic-slice_fusion.2
  32.0 0.6 fusion.36
  32.6 2.9 %bitcast_dynamic-update-slice_fusion.2 = f32[4,128,128]{2,1,0:T(8,128)} fusion(f32[4,128,128]{2,1,0:T(8,128)} %get-tuple-element.60, s32[]{:T(128)S(6)} %copy.17, f32[512,512]{1,0:T(8,128)} %get-tuple-element.63, s32[]{:T(128)} %bitcast.39, s32[]{:T(128)} %bitcast.40), kind=kLoop, calls=%fused_computation.clone.1 | loop fusion | bytes 132100 | tf_op jit(solution)/shard_map/jit(_solve_triangular)/triangular_solve
  35.6 40.1 %custom-call.4 = f32[4,128,128]{1,2,0:T(8,128)S(1)} custom-call(f32[4,128,128]{2,1,0:T(8,128)} %get-tuple-element.12), custom_call_target="InvertDiagBlocksLowerTriangular" | custom-call | tf_op jit(solution)/shard_map/jit(_solve_triangular)/triangular_solve | solution.py:149
  75.7 0.1 iota_compare_fusion
  75.8 0.1 fusion.11
  75.9 0.3 fusion.13
  76.2 1.2 convolution_subtract_fusion.2
  77.4 0.4 fusion.21
  77.9 1.3 convolution_subtract_fusion.1
  79.2 0.4 fusion.19
  79.6 1.6 convolution_subtract_fusion.3
  81.2 0.4 fusion.18
  81.6 1.0 pad_maximum_fusion.inverse_ref
  82.7 27.5 %all-to-all-done = f32[32,4,32,256]{3,2,1,0:T(8,128)} async-done(((f32[32,4,32,256]{3,2,1,0:T(8,128)}), f32[32,4,32,256]{3,2,1,0:T(8,128)}, u32[]{:S(2)}, u32[]{:S(2)}) %all-to-all-start) | async-done | bytes 4194336 | tf_op jit(solution)/shard_map/all_to_all | solution.py:140
  110.2 0.0 copy-start.3
  110.2 5.5 %copy.13 = f32[16,8,32,256]{3,1,2,0:T(8,128)S(1)} copy(f32[16,8,32,256]{3,2,1,0:T(8,128)} %bitcast.16) | data formatting | bytes 8388608
  115.7 0.0 copy-done.3
  115.7 0.0 copy-start.1
  115.7 1.3 fusion.22
  117.1 0.0 copy-start.2
  117.1 2.0 %copy-done.2 = f32[128,8192]{1,0:T(8,128)} copy-done((f32[128,8192]{1,0:T(8,128)}, f32[128,8192]{1,0:T(8,128)S(1)}, u32[]{:S(2)}) %copy-start.2) | copy-done | bytes 4194328
  119.1 0.0 copy-done.1
  119.1 33.4 %shard_map.55 = f32[128,1536]{1,0:T(8,128)S(1)} custom-call(f32[128,512]{1,0:T(8,128)S(1)} %slice.56.head_ref, f32[512,512]{1,0:T(8,128)S(1)} %copy-done.1, f32[512,1536]{1,0:T(8,128)S(1)} %slice.43.lead_ref), custom_call_target="tpu_custom_call" | custom-call | tf_op jit(solution)/shard_map/pallas_call | solution.py:103
  152.6 0.0 copy-start
  152.6 0.9 copy-done
  153.5 30.5 %convolution_subtract_fusion = f32[128,8192]{1,0:T(8,128)} fusion(f32[128,8192]{1,0:T(8,128)} %copy-done.2, f32[128,1536]{1,0:T(8,128)} %copy-done, f32[8192,1536]{1,0:T(8,128)} %param.9), kind=kOutput, calls=%fused_computation.2 | convolution fusion | flops 9664724992 | bytes 59506688 | tf_op jit(solution)/shard_map/dot_general | solution.py:157
  184.0 1.8 fusion.12
  (5 shorter events, 0.0 us)
Async XLA Ops:
  11.8 98.4 %all-to-all-start = ((f32[32,4,32,256]{3,2,1,0:T(8,128)}), f32[32,4,32,256]{3,2,1,0:T(8,128)}, u32[]{:S(2)}, u32[]{:S(2)}) async-start(f32[32,4,32,256]{3,2,1,0:T(8,128)} %bitcast.41), calls=%async_computation | async-start | bytes 8388608 | tf_op jit(solution)/shard_map/all_to_all | solution.py:140
  110.2 5.5 %copy-start.3 = (s32[1,128]{1,0:T(1,128)S(1)}, s32[1,128]{1,0:T(1,128)}, u32[]{:S(2)}) copy-start(s32[1,128]{1,0:T(1,128)} %param.8) | copy-start | bytes 1540
  115.7 3.4 %copy-start.1 = (f32[512,512]{1,0:T(8,128)S(1)}, f32[512,512]{1,0:T(8,128)}, u32[]{:S(2)}) copy-start(f32[512,512]{1,0:T(8,128)} %pad_maximum_fusion.inverse_ref) | copy-start | bytes 3145732
  117.1 2.0 %copy-start.2 = (f32[128,8192]{1,0:T(8,128)}, f32[128,8192]{1,0:T(8,128)S(1)}, u32[]{:S(2)}) copy-start(f32[128,8192]{1,0:T(8,128)S(1)} %fusion.22) | copy-start | bytes 12582916
  152.6 0.9 copy-start

commit v2 on v1

v2 whole, which is shorter than its diff:
```python
import functools

import jax
import jax.numpy as jnp
from jax import lax
from jax.experimental import pallas as pl
from jax.experimental.pallas import tpu as pltpu
from jax.sharding import PartitionSpec as P

PANEL = 512
PANELS = 3
CHUNKS = 4
SUB = 128
TILE = 256
TILE_SLOTS = 4
FIRST = 6
PER_STEP = 1
NT = (((1,), (1,)), ((), ()))


def dot_exact(a, b):
    return lax.dot_general(
        a, b, NT, precision=lax.Precision.HIGHEST, preferred_element_type=jnp.float32
    )


def mega_kernel(
    n_feat, n_pair, pad, heads_ref, place_ref, lead_ref, factor_ref, outgoing_ref,
    received_ref, update_ref, solved_ref,
    arrived, inverse, current, held, split, tiles,
    head_send, head_recv, chain_send, chain_recv, swap_send, swap_recv, own_sem, tile_sem,
):
    feat = lax.axis_index("feat")
    pair = lax.axis_index("pair")
    devices = n_feat * n_pair
    me = feat * n_pair + pair
    level = feat // 2
    levels = n_feat // 2
    parity = lax.rem(feat, 2)
    partner = feat + 1 - 2 * parity
    pairs = held.shape[0]
    rows = pairs // CHUNKS
    depth = PANELS * PANEL

    def remote(src, dst, send_sem, recv_sem, target):
        return pltpu.make_async_remote_copy(
            src_ref=src,
            dst_ref=dst,
            send_sem=send_sem,
            recv_sem=recv_sem,
            device_id=target,
            device_id_type=pl.DeviceIdType.MESH,
        )

    def tile_copy(t, slot):
        return pltpu.make_async_copy(
            factor_ref.at[pl.ds(t * TILE, TILE), :], tiles.at[slot], tile_sem.at[slot]
        )

    tile_count = factor_ref.shape[0] // TILE
    depth_ahead = min(TILE_SLOTS, tile_count)
    for t in range(depth_ahead):
        tile_copy(t, t).start()

    barrier = pltpu.get_barrier_semaphore()

    def greet(j, carry):
        target = lax.rem(me + j, devices)
        pl.semaphore_signal(
            barrier,
            inc=1,
            device_id=(target // n_pair, lax.rem(target, n_pair)),
            device_id_type=pl.DeviceIdType.MESH,
        )
        return carry

    lax.fori_loop(1, devices, greet, 0)
    pl.semaphore_wait(barrier, devices - 1)

    mine = pl.ds(pl.multiple_of(me * pad, pad), pad)

    def head_copy(k, b):
        at = k * n_pair + b
        return remote(
            heads_ref.at[pl.ds(at * pad, pad), :],
            arrived.at[mine, :],
            head_send.at[at],
            head_recv.at[me],
            (k, b),
        )

    for k in range(PANELS):
        for b in range(n_pair):

            @pl.when(me != k * n_pair + b)
            def _():
                head_copy(k, b).start()

    own_copy = pltpu.make_async_copy(outgoing_ref.at[me], received_ref.at[me], own_sem)
    own_copy.start()

    def swap(i):
        step = i + 1 if i >= devices - n_pair else i
        ring = step // n_pair
        shift = n_feat // 2 + (ring + 1) // 2 * (2 * (ring % 2) - 1)
        to_feat = lax.rem(feat + shift, n_feat)
        to_pair = lax.rem(pair + step % n_pair, n_pair)
        target = to_feat * n_pair + to_pair
        return remote(
            outgoing_ref.at[target],
            received_ref.at[me],
            swap_send.at[i],
            swap_recv.at[me],
            (to_feat, to_pair),
        )

    swaps = devices - 1
    issued = 0

    def issue(count):
        nonlocal issued
        for i in range(issued, min(issued + count, swaps)):
            swap(i).start()
        issued = min(issued + count, swaps)

    issue(FIRST)
    subs = PANEL // SUB

    @pl.when(feat < PANELS)
    def _():
        column = pl.multiple_of(feat * PANEL, PANEL)
        lines = lax.broadcasted_iota(jnp.int32, (SUB, SUB), 0)
        lanes = lax.broadcasted_iota(jnp.int32, (SUB, SUB), 1)
        eye = jnp.where(lines == lanes, 1.0, 0.0).astype(jnp.float32)
        for s in range(subs):
            inverse[s] = eye

        def group(g, work):
            base = pl.multiple_of(g * 8, 8)
            for r in range(8):
                for s in range(subs):
                    col = work[s][:, r : r + 1]
                    block = inverse[s, pl.ds(base, 8), :]
                    pivot = jnp.sum(
                        jnp.where(lines[:, :1] == base + r, col, 0.0), axis=0, keepdims=True
                    )
                    row = block[r : r + 1, :] / pivot
                    below = jnp.where(lines[:, :1] > base + r, col, 0.0)
                    old = inverse[s]
                    inverse[s] = jnp.where(lines == base + r, row, old - below * row)
            return tuple(pltpu.roll(w, SUB - 8, 1) for w in work)

        start = tuple(
            lead_ref[s * SUB : (s + 1) * SUB, pl.ds(column + s * SUB, SUB)] for s in range(subs)
        )
        lax.fori_loop(0, SUB // 8, group, start)

        own_head = pl.multiple_of((feat * n_pair + pair) * pad, pad)
        arrived[mine, :] = heads_ref[pl.ds(own_head, pad), :]

        def take(j, carry):
            source = lax.rem(me + j, devices)
            part = arrived.at[pl.ds(pl.multiple_of(source * pad, pad), pad), :]
            remote(part, part, head_send.at[0], head_recv.at[source], (feat, pair)).wait_recv()
            return carry

        lax.fori_loop(1, devices, take, 0)
        current[...] = jnp.dot(
            place_ref[...],
            arrived[...],
            precision=lax.Precision.HIGHEST,
            preferred_element_type=jnp.float32,
        )

    def piece(k, c, way, target):
        part = held.at[pl.ds(c * rows, rows), pl.ds(k * PANEL, PANEL)]
        return remote(
            part, part, chain_send.at[k, c, way], chain_recv.at[k, c], (target, pair)
        )

    def routes(k, c):
        top = k // 2
        side = k % 2 if c < CHUNKS // 2 else 1 - k % 2
        on_side = parity == side
        return (
            (0, (feat == k) | (on_side & (level != top)), partner),
            (1, on_side & (level >= top) & (level + 1 < levels), feat + 2),
            (2, on_side & (level <= top) & (level > 0), feat - 2),
        )

    for k in range(PANELS):

        @pl.when(feat == k)
        def _():
            left = current[...]
            if k > 0:
                left = left - dot_exact(held[:, : k * PANEL], lead_ref[:, : k * PANEL])
            for s in range(subs):
                part = left[:, s * SUB : (s + 1) * SUB]
                if s > 0:
                    part = part - dot_exact(
                        held[:, k * PANEL : k * PANEL + s * SUB],
                        lead_ref[s * SUB : (s + 1) * SUB, k * PANEL : k * PANEL + s * SUB],
                    )
                held[:, k * PANEL + s * SUB : k * PANEL + (s + 1) * SUB] = dot_exact(
                    part, inverse[s]
                )

        for c in range(CHUNKS):

            @pl.when(feat != k)
            def _():
                piece(k, c, 0, partner).wait_recv()

            for way, active, target in routes(k, c):

                @pl.when(active)
                def _():
                    piece(k, c, way, target).start()

            issue(PER_STEP)

    issue(swaps)
    whole = held[...]
    high = whole.astype(jnp.bfloat16)
    split[:pairs, :] = high
    split[pairs:, :] = (whole - high.astype(jnp.float32)).astype(jnp.bfloat16)
    solved_ref[...] = whole

    def multiply(t, carry):
        slot = lax.rem(t, depth_ahead)
        tile_copy(t, slot).wait()
        tile = tiles[slot]
        top = tile.astype(jnp.bfloat16)
        low = (tile - top.astype(jnp.float32)).astype(jnp.bfloat16)
        both = lax.dot_general(split[...], top, NT, preferred_element_type=jnp.float32)
        rest = lax.dot_general(split[:pairs, :], low, NT, preferred_element_type=jnp.float32)
        columns = pl.ds(pl.multiple_of(t * TILE, TILE), TILE)
        update_ref[:, columns] = both[:pairs] + (both[pairs:] + rest)

        @pl.when(t + depth_ahead < tile_count)
        def _():
            tile_copy(t + depth_ahead, slot).start()

        return carry

    lax.fori_loop(0, tile_count, multiply, 0)

    for k in range(PANELS):
        for b in range(n_pair):

            @pl.when(me != k * n_pair + b)
            def _():
                head_copy(k, b).wait_send()

        for c in range(CHUNKS):
            for way, active, target in routes(k, c):

                @pl.when(active)
                def _():
                    piece(k, c, way, target).wait_send()

    own_copy.wait()
    for i in range(swaps):
        swap(i).wait_send()

    def collect(j, carry):
        source = lax.rem(me + j, devices)
        part = received_ref.at[source]
        remote(part, part, swap_send.at[0], swap_recv.at[source], (feat, pair)).wait_recv()
        return carry

    lax.fori_loop(1, devices, collect, 0)


def exchange_and_solve(heads, place, lead, factor_panels, outgoing, n_feat, n_pair, pad):
    pairs = place.shape[0]
    devices = n_feat * n_pair
    vmem = pl.BlockSpec(memory_space=pltpu.VMEM)
    anywhere = pl.BlockSpec(memory_space=pl.ANY)
    dma = pltpu.SemaphoreType.DMA
    return pl.pallas_call(
        functools.partial(mega_kernel, n_feat, n_pair, pad),
        out_shape=(
            jax.ShapeDtypeStruct(outgoing.shape, jnp.float32),
            jax.ShapeDtypeStruct((pairs, factor_panels.shape[0]), jnp.float32),
            jax.ShapeDtypeStruct((pairs, PANELS * PANEL), jnp.float32),
        ),
        in_specs=[vmem, vmem, vmem, anywhere, anywhere],
        out_specs=(anywhere, vmem, vmem),
        scratch_shapes=[
            pltpu.VMEM((devices * pad, PANEL), jnp.float32),
            pltpu.VMEM((PANEL // SUB, SUB, SUB), jnp.float32),
            pltpu.VMEM((pairs, PANEL), jnp.float32),
            pltpu.VMEM((pairs, PANELS * PANEL), jnp.float32),
            pltpu.VMEM((2 * pairs, PANELS * PANEL), jnp.bfloat16),
            pltpu.VMEM((TILE_SLOTS, TILE, PANELS * PANEL), jnp.float32),
            dma((PANELS * n_pair,)),
            dma((devices,)),
            dma((PANELS, CHUNKS, 3)),
            dma((PANELS, CHUNKS)),
            dma((devices,)),
            dma((devices,)),
            dma,
            dma((TILE_SLOTS,)),
        ],
        compiler_params=pltpu.CompilerParams(
            collective_id=0, has_side_effects=True, vmem_limit_bytes=56 * 1024 * 1024
        ),
    )(heads, place, lead, factor_panels, outgoing)


def per_device(in_factors, out_factors, token_counts, slot_pair, factor_panels):
    slot_count, side_count, token_depth, proj_rank = in_factors.shape
    n_pair = lax.axis_size("pair")
    n_feat = lax.axis_size("feat")
    per_group = slot_count // n_pair
    row_count = factor_panels.shape[0]
    block = row_count // proj_rank
    feat_index = lax.axis_index("feat")
    positions = lax.broadcasted_iota(jnp.int32, (slot_count, side_count, token_depth), 2)
    side_index = lax.broadcasted_iota(jnp.int32, (slot_count, side_count, token_depth), 1)
    weights = jnp.where(
        positions < token_counts[:, :, None], jnp.where(side_index == 0, 1.0, -1.0), 0.0
    ).astype(jnp.bfloat16)
    signed = out_factors * weights[..., None]
    gradients = jnp.einsum("ksti,kstj->kij", signed, in_factors, preferred_element_type=jnp.float32)
    gradients = gradients.reshape(n_pair, per_group, n_feat, block, proj_rank)
    group_pairs = slot_pair[0]
    pair_total = n_pair * n_feat * per_group
    outgoing = gradients.transpose(2, 0, 1, 3, 4).reshape(
        n_feat * n_pair, per_group, block, proj_rank
    )
    pad = -(-per_group // 8) * 8
    slim = PANEL // proj_rank
    heads = jnp.stack([gradients[:, :, k, :slim, :] for k in range(PANELS)])
    heads = heads.reshape(PANELS, n_pair, per_group, PANEL)
    heads = jnp.pad(heads, ((0, 0), (0, 0), (0, pad - per_group), (0, 0)))
    heads = heads.reshape(PANELS * n_pair * pad, PANEL)
    spots = jnp.pad(
        group_pairs.reshape(n_feat * n_pair, per_group),
        ((0, 0), (0, pad - per_group)),
        constant_values=-1,
    ).reshape(-1)
    wide_rows = lax.broadcasted_iota(jnp.int32, (pair_total, spots.shape[0]), 0)
    place = (wide_rows == spots[None, :]).astype(jnp.float32)
    received, update, solved = exchange_and_solve(
        heads, place, factor_panels[:PANEL], factor_panels, outgoing, n_feat, n_pair, pad
    )
    received = received.reshape(pair_total, row_count)
    pair_rows = lax.broadcasted_iota(jnp.int32, (pair_total, pair_total), 0)
    placement = (pair_rows == group_pairs[None, :]).astype(jnp.float32)
    result = (
        jnp.dot(
            placement, received, precision=lax.Precision.HIGH, preferred_element_type=jnp.float32
        )
        - update
    )
    own = jnp.minimum(feat_index, PANELS - 1)
    own_solved = lax.dynamic_slice(solved, (0, own * PANEL), (pair_total, PANEL))
    head = jnp.where(feat_index < PANELS, own_solved, result[:, :PANEL])
    return lax.dynamic_update_slice(result, head, (0, 0))


def solution(mesh):
    return jax.shard_map(
        per_device,
        mesh=mesh,
        in_specs=(
            P(("feat", "pair"), None, None, None),
            P(("feat", "pair"), None, None, None),
            P(("feat", "pair"), None),
            P("pair", None),
            P("feat", None),
        ),
        out_specs=P("pair", "feat"),
        check_vma=False,
    )
```

time: 189 us -> 174 us (0.921); the launches traced: 186 us -> 174 us
  Pallas kernels: 33.4 us -> 140 us
  other arithmetic: 44.3 us -> 3.85 us
  matrix products: 46.1 us -> 12.1 us
  waiting for transfers between devices: 27.5 us -> 0 us
  local copies, waits for them, and re-layouts: 28.2 us -> 17.7 us
  starting transfers between devices: 5.93 us -> 0 us
    pallas_call x1, Pallas kernels: 33.4 us -> 140 us  [exchange_and_solve(): pl.pallas_call(functools.partial(mega_kernel, n_feat, n_pair, pad), out_s...]
    another operation x4 -> x1, other arithmetic: 42.3 us -> 0.72 us  [per_device(): heads = jnp.stack([gradients[:, :, k, :slim, :] for k in range(PANELS)])]
    dot_general x1 -> x0, matrix products: 30.5 us -> none  [per_device(): lax.dot_general(solved, factor_panels, NT, precision=lax.Precision.HIGH,...]
    all_to_all x1 -> x0, waiting for transfers between devices: 27.5 us -> none  [per_device(): lax.all_to_all(outgoing, ('feat', 'pair'), split_axis=0, concat_axis=1, t...]
    another operation x13 -> x4, local copies, waits for them, and re-layouts: 14.6 us -> 0.2 us  [the longest x3 0.1 us: per_device(): heads = jnp.stack([gradients[:, :, k, :slim, :] for k in range(PANELS)])]
    all_to_all x1 -> x0, starting transfers between devices: 5.93 us -> none  [per_device(): lax.all_to_all(outgoing, ('feat', 'pair'), split_axis=0, concat_axis=1, t...]
    another operation x7 -> x0, matrix products: 5.67 us -> none  [per_device(): inverse = jax.scipy.linalg.solve_triangular(diagonal, identity, lower=True)]
    reshape x1, local copies, waits for them, and re-layouts: 2.35 us -> 4.71 us  [per_device(): gradients = gradients.reshape(n_pair, per_group, n_feat, block, proj_rank)]
  transfers between devices with their start and end apart: 1 -> 0, of which waited for: 1 -> 0; matrix products, arithmetic and copies ran while one was open for 35% -> 0% of each run, Pallas kernels for 0% -> 0%
where the time goes in v2:
time: 174 us
  Pallas kernels  140 us (80%)
  local copies, waits for them, and re-layouts  17.7 us (10%)
  matrix products  12.1 us (7%)
  other arithmetic  3.85 us (2%)
    pallas_call x1, Pallas kernels, exchange_and_solve(): pl.pallas_call(functools.partial(mega_kernel, n_feat, n_pair, pad), out_s...  140 us
    unnamed x9, local copies, waits for them, and re-layouts  8.93 us
    dot_general x1, matrix products, per_device(): jnp.einsum('ksti,kstj->kij', signed, in_factors, preferred_element_type=j...  8.54 us
    reshape x1, local copies, waits for them, and re-layouts, per_device(): gradients = gradients.reshape(n_pair, per_group, n_feat, block, proj_rank)  4.71 us
    slice x1, local copies, waits for them, and re-layouts, per_device(): factor_panels[:PANEL]  3.77 us
    dot_general x1, matrix products, per_device(): jnp.dot(placement, received, precision=lax.Precision.HIGH, preferred_elem...  3.53 us

profile of v2, /device:TPU:24, one launch (start us, length us, event | category | flops | bytes accessed | tf_op | source)
XLA Modules:
  0.0 174.1 jit_solution(5660218462892004875)
XLA Ops:
  0.0 0.8 copy.9
  0.8 0.1 fusion.5
  0.9 8.5 %fusion = f32[16,256,256,1]{2,1,3,0:T(8,128)S(1)} fusion(bf16[16,2,512,256]{3,2,1,0:T(8,128)(2,1)} %param.5, bf16[16,2,512,256]{3,2,1,0:T(8,128)(2,1)} %param.6, bf16[16,2,512]{2,1,0:T(2,128)(2,1)S(1)} %fusion.5), kind=kOutput, calls=%fused_computation.1 | convolution fusion | flops 2151677952 | bytes 21004288 | tf_op jit(solution)/shard_map/ksti,kstj->kij/dot_general | solution.py:327
  9.4 0.0 copy-start
  9.4 2.0 %copy-done = f32[16,256,256,1]{2,1,3,0:T(8,128)} copy-done((f32[16,256,256,1]{2,1,3,0:T(8,128)}, f32[16,256,256,1]{2,1,3,0:T(8,128)S(1)}, u32[]{:S(2)}) %copy-start) | copy-done | bytes 4194328
  11.6 0.7 select_maximum_fusion
  12.3 4.7 %copy.11 = f32[4,4,8,32,256]{4,3,1,0,2:T(8,128)} copy(f32[4,4,8,32,256]{4,3,2,1,0:T(8,128)} %bitcast.17) | data formatting | bytes 8388608 | tf_op jit(solution)/shard_map/reshape | solution.py:328
  17.0 0.0 copy-start.2
  17.0 3.8 %slice.18.lead_ref = f32[512,1536]{1,0:T(8,128)} slice(f32[8192,1536]{1,0:T(8,128)} %factor_ref.1), slice={[0:512], [0:1536]} | slice | bytes 6291456 | tf_op jit(solution)/shard_map/slice | solution.py:348
  20.8 0.5 broadcast.35
  21.3 0.0 copy-done.2
  21.3 0.6 reduce.3
  21.9 0.1 reshape_squeeze.3
  22.0 0.1 eq.32
  22.1 0.7 fusion.4.place_ref
  22.8 140.4 %shard_map.55 = (f32[32,4,32,256]{3,2,1,0:T(8,128)}, f32[128,8192]{1,0:T(8,128)}, f32[128,1536]{1,0:T(8,128)}) custom-call(f32[96,512]{1,0:T(8,128)} %bitcast.19, f32[128,256]{1,0:T(8,128)} %fusion.4.place_ref, f32[512,1536]{1,0:T(8,128)} %slice.18.lead_ref, f32[8192,1536]{1,0:T(8,128)} %factor_ref.1, f32[32,4,32,256]{3,2,1,0:T(8,128)} %bitcast.15), custom_call_target="tpu_custom_call" | custom-call | tf_op jit(solution)/shard_map/pallas_call | solution.py:282
  163.1 0.0 copy-start.1
  163.1 5.7 %copy.14 = f32[16,8,32,256]{3,1,2,0:T(8,128)S(1)} copy(f32[16,8,32,256]{3,2,1,0:T(8,128)} %bitcast.18) | data formatting | bytes 8388608
  168.8 0.0 copy-done.1
  168.8 3.5 %convolution_subtract_fusion = f32[128,8192]{1,0:T(8,128)} fusion(f32[128,8192]{1,0:T(8,128)S(1)} %copy-done.1, f32[128,8192]{1,0:T(8,128)S(1)} %bitcast.14, s32[128]{0:T(128)S(1)} %bitcast.20), kind=kOutput, calls=%fused_computation | convolution fusion | flops 806371328 | bytes 12583424 | tf_op jit(solution)/shard_map/dot_general | solution.py:354
  172.3 1.8 %fusion.3 = f32[128,8192]{1,0:T(8,128)} fusion(f32[128,8192]{1,0:T(8,128)} %convolution_subtract_fusion, f32[128,1536]{1,0:T(8,128)} %get-tuple-element.10, s32[]{:T(128)S(6)} %select_n.28, pred[]{:T(512)S(6)} %lt.20), kind=kLoop, calls=%fused_computation.5 | loop fusion | flops 65536 | bytes 786437 | tf_op jit(solution)/shard_map/dynamic_update_slice | solution.py:362
  (6 shorter events, 0.1 us)
Async XLA Ops:
  9.4 2.0 %copy-start = (f32[16,256,256,1]{2,1,3,0:T(8,128)}, f32[16,256,256,1]{2,1,3,0:T(8,128)S(1)}, u32[]{:S(2)}) copy-start(f32[16,256,256,1]{2,1,3,0:T(8,128)S(1)} %fusion) | copy-start | bytes 12582916
  17.0 4.3 %copy-start.2 = (s32[1,128]{1,0:T(1,128)S(1)}, s32[1,128]{1,0:T(1,128)}, u32[]{:S(2)}) copy-start(s32[1,128]{1,0:T(1,128)} %param.8) | copy-start | bytes 1540
  163.1 5.7 %copy-start.1 = (f32[128,8192]{1,0:T(8,128)S(1)}, f32[128,8192]{1,0:T(8,128)}, u32[]{:S(2)}) copy-start(f32[128,8192]{1,0:T(8,128)} %get-tuple-element.9) | copy-start | bytes 12582916

commit v3 on v2

--- a/solution.py
+++ b/solution.py
@@ -25,10 +25,10 @@
 
 
 def mega_kernel(
-    n_feat, n_pair, pad, heads_ref, place_ref, lead_ref, factor_ref, outgoing_ref,
+    n_feat, n_pair, pad, heads_ref, place_ref, factor_ref, outgoing_ref,
     received_ref, update_ref, solved_ref,
-    arrived, inverse, current, held, split, tiles,
-    head_send, head_recv, chain_send, chain_recv, swap_send, swap_recv, own_sem, tile_sem,
+    arrived, inverse, current, held, split, tiles, lead_ref,
+    head_send, head_recv, chain_send, chain_recv, swap_send, swap_recv, own_sem, tile_sem, lead_sem,
 ):
     feat = lax.axis_index("feat")
     pair = lax.axis_index("pair")
@@ -57,6 +57,8 @@
             factor_ref.at[pl.ds(t * TILE, TILE), :], tiles.at[slot], tile_sem.at[slot]
         )
 
+    lead_copy = pltpu.make_async_copy(factor_ref.at[pl.ds(0, PANEL), :], lead_ref, lead_sem)
+    lead_copy.start()
     tile_count = factor_ref.shape[0] // TILE
     depth_ahead = min(TILE_SLOTS, tile_count)
     for t in range(depth_ahead):
@@ -96,7 +98,16 @@
             def _():
                 head_copy(k, b).start()
 
-    own_copy = pltpu.make_async_copy(outgoing_ref.at[me], received_ref.at[me], own_sem)
+    per_group, block = received_ref.shape[1:3]
+
+    def parcel(to_feat, to_pair):
+        return outgoing_ref.at[
+            pl.ds(to_pair * per_group, per_group),
+            pl.ds(pl.multiple_of(to_feat * block, block), block),
+            :,
+        ]
+
+    own_copy = pltpu.make_async_copy(parcel(feat, pair), received_ref.at[me], own_sem)
     own_copy.start()
 
     def swap(i):
@@ -105,9 +116,8 @@
         shift = n_feat // 2 + (ring + 1) // 2 * (2 * (ring % 2) - 1)
         to_feat = lax.rem(feat + shift, n_feat)
         to_pair = lax.rem(pair + step % n_pair, n_pair)
-        target = to_feat * n_pair + to_pair
         return remote(
-            outgoing_ref.at[target],
+            parcel(to_feat, to_pair),
             received_ref.at[me],
             swap_send.at[i],
             swap_recv.at[me],
@@ -124,6 +134,7 @@
         issued = min(issued + count, swaps)
 
     issue(FIRST)
+    lead_copy.wait()
     subs = PANEL // SUB
 
     @pl.when(feat < PANELS)
@@ -273,8 +284,10 @@
     lax.fori_loop(1, devices, collect, 0)
 
 
-def exchange_and_solve(heads, place, lead, factor_panels, outgoing, n_feat, n_pair, pad):
+def exchange_and_solve(heads, place, factor_panels, outgoing, n_feat, n_pair, pad):
     pairs = place.shape[0]
+    block = factor_panels.shape[0] // outgoing.shape[2]
+    per_group = outgoing.shape[0] // n_pair
     devices = n_feat * n_pair
     vmem = pl.BlockSpec(memory_space=pltpu.VMEM)
     anywhere = pl.BlockSpec(memory_space=pl.ANY)
@@ -282,11 +295,13 @@
     return pl.pallas_call(
         functools.partial(mega_kernel, n_feat, n_pair, pad),
         out_shape=(
-            jax.ShapeDtypeStruct(outgoing.shape, jnp.float32),
+            jax.ShapeDtypeStruct(
+                (devices, per_group, block, outgoing.shape[2]), jnp.float32
+            ),
             jax.ShapeDtypeStruct((pairs, factor_panels.shape[0]), jnp.float32),
             jax.ShapeDtypeStruct((pairs, PANELS * PANEL), jnp.float32),
         ),
-        in_specs=[vmem, vmem, vmem, anywhere, anywhere],
+        in_specs=[vmem, vmem, anywhere, anywhere],
         out_specs=(anywhere, vmem, vmem),
         scratch_shapes=[
             pltpu.VMEM((devices * pad, PANEL), jnp.float32),
@@ -295,6 +310,7 @@
             pltpu.VMEM((pairs, PANELS * PANEL), jnp.float32),
             pltpu.VMEM((2 * pairs, PANELS * PANEL), jnp.bfloat16),
             pltpu.VMEM((TILE_SLOTS, TILE, PANELS * PANEL), jnp.float32),
+            pltpu.VMEM((PANEL, PANELS * PANEL), jnp.float32),
             dma((PANELS * n_pair,)),
             dma((devices,)),
             dma((PANELS, CHUNKS, 3)),
@@ -303,11 +319,51 @@
             dma((devices,)),
             dma,
             dma((TILE_SLOTS,)),
+            dma,
         ],
         compiler_params=pltpu.CompilerParams(
             collective_id=0, has_side_effects=True, vmem_limit_bytes=56 * 1024 * 1024
         ),
-    )(heads, place, lead, factor_panels, outgoing)
+    )(heads, place, factor_panels, outgoing)
+
+
+def finish_kernel(slim, keep_ref, placement_ref, own_ref, received_ref, update_ref, out_ref):
+    rank = received_ref.shape[2]
+    step = pl.program_id(0)
+    placement = placement_ref[...]
+    for i in range(received_ref.shape[1]):
+        slab = received_ref[:, i, :]
+        high = slab.astype(jnp.bfloat16)
+        low = (slab - high.astype(jnp.float32)).astype(jnp.bfloat16)
+        placed = jnp.dot(placement, high, preferred_element_type=jnp.float32) + jnp.dot(
+            placement, low, preferred_element_type=jnp.float32
+        )
+        columns = slice(i * rank, (i + 1) * rank)
+        value = placed - update_ref[:, columns]
+        if i < slim:
+            owner = (keep_ref[0:1, 0:1] > 0.5) & (step == 0)
+            value = jnp.where(owner, own_ref[:, columns], value)
+        out_ref[:, columns] = value
+
+
+def place_and_subtract(received, placement, update, own_solved, keep):
+    pairs, block, rank = received.shape
+    vmem = pl.BlockSpec(memory_space=pltpu.VMEM)
+    lines = 8
+    return pl.pallas_call(
+        functools.partial(finish_kernel, PANEL // rank),
+        grid=(block // lines,),
+        out_shape=jax.ShapeDtypeStruct(update.shape, jnp.float32),
+        in_specs=[
+            vmem,
+            vmem,
+            vmem,
+            pl.BlockSpec((pairs, lines, rank), lambda t: (0, t, 0)),
+            pl.BlockSpec((pairs, lines * rank), lambda t: (0, t)),
+        ],
+        out_specs=pl.BlockSpec((pairs, lines * rank), lambda t: (0, t)),
+        compiler_params=pltpu.CompilerParams(vmem_limit_bytes=56 * 1024 * 1024),
+    )(keep, placement, own_solved, received, update)
 
 
 def per_device(in_factors, out_factors, token_counts, slot_pair, factor_panels):
@@ -325,12 +381,10 @@
     ).astype(jnp.bfloat16)
     signed = out_factors * weights[..., None]
     gradients = jnp.einsum("ksti,kstj->kij", signed, in_factors, preferred_element_type=jnp.float32)
+    outgoing = gradients
     gradients = gradients.reshape(n_pair, per_group, n_feat, block, proj_rank)
     group_pairs = slot_pair[0]
     pair_total = n_pair * n_feat * per_group
-    outgoing = gradients.transpose(2, 0, 1, 3, 4).reshape(
-        n_feat * n_pair, per_group, block, proj_rank
-    )
     pad = -(-per_group // 8) * 8
     slim = PANEL // proj_rank
     heads = jnp.stack([gradients[:, :, k, :slim, :] for k in range(PANELS)])
@@ -345,21 +399,16 @@
     wide_rows = lax.broadcasted_iota(jnp.int32, (pair_total, spots.shape[0]), 0)
     place = (wide_rows == spots[None, :]).astype(jnp.float32)
     received, update, solved = exchange_and_solve(
-        heads, place, factor_panels[:PANEL], factor_panels, outgoing, n_feat, n_pair, pad
-    )
-    received = received.reshape(pair_total, row_count)
-    pair_rows = lax.broadcasted_iota(jnp.int32, (pair_total, pair_total), 0)
-    placement = (pair_rows == group_pairs[None, :]).astype(jnp.float32)
-    result = (
-        jnp.dot(
-            placement, received, precision=lax.Precision.HIGH, preferred_element_type=jnp.float32
-        )
-        - update
+        heads, place, factor_panels, outgoing, n_feat, n_pair, pad
     )
     own = jnp.minimum(feat_index, PANELS - 1)
     own_solved = lax.dynamic_slice(solved, (0, own * PANEL), (pair_total, PANEL))
-    head = jnp.where(feat_index < PANELS, own_solved, result[:, :PANEL])
-    return lax.dynamic_update_slice(result, head, (0, 0))
+    keep = jnp.broadcast_to((feat_index < PANELS).astype(jnp.float32), (8, 128))
+    pair_rows = lax.broadcasted_iota(jnp.int32, (pair_total, pair_total), 0)
+    placement = (pair_rows == group_pairs[None, :]).astype(jnp.bfloat16)
+    return place_and_subtract(
+        received.reshape(pair_total, block, proj_rank), placement, update, own_solved, keep
+    )
 
 
 def solution(mesh):

time: 174 us -> 173 us (level)
  Pallas kernels: 140 us -> 156 us
  local copies, waits for them, and re-layouts: 17.7 us -> 5.9 us
  matrix products: 12.1 us -> 8.54 us
    pallas_call x0 -> x1, Pallas kernels: none -> 16.8 us  [place_and_subtract(): pl.pallas_call(functools.partial(finish_kernel, PANEL // rank), grid=(blo...]
    unnamed x9 -> x6, local copies, waits for them, and re-layouts: 8.93 us -> 3.31 us
    reshape x1 -> x0, local copies, waits for them, and re-layouts: 4.71 us -> none  [per_device(): gradients = gradients.reshape(n_pair, per_group, n_feat, block, proj_rank)]
    slice x1 -> x0, local copies, waits for them, and re-layouts: 3.77 us -> none  [per_device(): factor_panels[:PANEL]]
    dot_general x1 -> x0, matrix products: 3.53 us -> none  [per_device(): jnp.dot(placement, received, precision=lax.Precision.HIGH, preferred_elem...]
    dynamic_update_slice x1 -> x0, other arithmetic: 1.77 us -> none  [per_device(): return lax.dynamic_update_slice(result, head, (0, 0))]
where the time goes in v3:
time: 173 us
  Pallas kernels  156 us (90%)
  matrix products  8.54 us (5%)
  local copies, waits for them, and re-layouts  5.9 us (3%)
  other arithmetic  2.78 us (2%)
    pallas_call x1, Pallas kernels, exchange_and_solve(): pl.pallas_call(functools.partial(mega_kernel, n_feat, n_pair, pad), out_s...  139 us
    pallas_call x1, Pallas kernels, place_and_subtract(): pl.pallas_call(functools.partial(finish_kernel, PANEL // rank), grid=(blo...  16.8 us
    dot_general x1, matrix products, per_device(): jnp.einsum('ksti,kstj->kij', signed, in_factors, preferred_element_type=j...  8.54 us

profile of v3, /device:TPU:24, one launch (start us, length us, event | category | flops | bytes accessed | tf_op | source)
XLA Modules:
  0.0 173.1 jit_solution(2951651164415409652)
XLA Ops:
  0.0 0.8 copy.8
  0.8 0.1 fusion.4
  0.9 0.0 copy-start.1
  0.9 8.5 %fusion = f32[16,256,256,1]{2,1,3,0:T(8,128)S(1)} fusion(bf16[16,2,512,256]{3,2,1,0:T(8,128)(2,1)} %param.5, bf16[16,2,512,256]{3,2,1,0:T(8,128)(2,1)} %param.6, bf16[16,2,512]{2,1,0:T(2,128)(2,1)S(1)} %fusion.4), kind=kOutput, calls=%fused_computation | convolution fusion | flops 2151677952 | bytes 21004288 | tf_op jit(solution)/shard_map/ksti,kstj->kij/dot_general | solution.py:383
  9.4 0.0 copy-start
  9.4 2.0 %copy-done = f32[16,256,256,1]{2,1,3,0:T(8,128)} copy-done((f32[16,256,256,1]{2,1,3,0:T(8,128)}, f32[16,256,256,1]{2,1,3,0:T(8,128)S(1)}, u32[]{:S(2)}) %copy-start) | copy-done | bytes 4194328
  11.6 0.7 select_maximum_fusion
  12.3 0.5 broadcast.35
  12.9 0.0 copy-done.1
  12.9 0.7 reduce.3
  13.5 0.1 reshape_squeeze.3
  13.6 0.1 eq.32
  13.7 0.7 fusion.3.place_ref
  14.4 139.1 %shard_map.55 = (f32[32,4,32,256]{3,2,1,0:T(8,128)}, f32[128,8192]{1,0:T(8,128)}, f32[128,1536]{1,0:T(8,128)}) custom-call(f32[96,512]{1,0:T(8,128)} %bitcast.11, f32[128,256]{1,0:T(8,128)} %fusion.3.place_ref, f32[8192,1536]{1,0:T(8,128)} %factor_ref.1, f32[16,256,256]{2,1,0:T(8,128)} %bitcast.9), custom_call_target="tpu_custom_call" | custom-call | tf_op jit(solution)/shard_map/pallas_call | solution.py:295
  153.5 1.7 constant_dynamic-slice_fusion.own_ref
  155.2 0.6 broadcast_in_dim.17.keep_ref
  155.7 0.6 fusion.5.placement_ref
  156.4 16.8 %shard_map.56 = f32[128,8192]{1,0:T(8,128)} custom-call(f32[8,128]{1,0:T(8,128)} %broadcast_in_dim.17.keep_ref, bf16[128,128]{1,0:T(8,128)(2,1)} %fusion.5.placement_ref, f32[128,512]{1,0:T(8,128)} %constant_dynamic-slice_fusion.own_ref, f32[128,32,256]{2,1,0:T(8,128)} %bitcast.10, f32[128,8192]{1,0:T(8,128)} %get-tuple-element.10.update_ref), custom_call_target="tpu_custom_call" | custom-call | tf_op jit(solution)/shard_map/pallas_call | solution.py:353
  (6 shorter events, 0.1 us)
Async XLA Ops:
  0.9 12.0 %copy-start.1 = (s32[1,128]{1,0:T(1,128)S(1)}, s32[1,128]{1,0:T(1,128)}, u32[]{:S(2)}) copy-start(s32[1,128]{1,0:T(1,128)} %param.8) | copy-start | bytes 1540
  9.4 2.0 %copy-start = (f32[16,256,256,1]{2,1,3,0:T(8,128)}, f32[16,256,256,1]{2,1,3,0:T(8,128)S(1)}, u32[]{:S(2)}) copy-start(f32[16,256,256,1]{2,1,3,0:T(8,128)S(1)} %fusion) | copy-start | bytes 12582916
